TPU v7x, 128 devices: a whole 4x4x4 slice. The times are simulated.
128 devices in a mesh: row: 8 (over z, core), col: 16 (over y, x).
Axes of the slice: x: 4, y: 4, z: 4, core: 2. Of those that a mesh axis runs over, the one named last changes fastest.
Arguments:
- emb: bfloat16 [524288, 512], P(('row', 'col')), may hold values from -6 to 6
- tiles: bfloat16 [2048, 4, 256, 256], P(('row', 'col')), may hold values from -0.375 to 0.375
- msg_src: int32 [2048, 4], P(('row', 'col')), may hold values from 0 to 15
- msg_dst: int32 [2048, 4], P(('row', 'col')), may hold values from 0 to 16, as said below
- msg_count: int32 [2048, 4], P(('row', 'col')), may hold values from 1 to 256
- weight: bfloat16 [512, 512], replicated, may hold values from -0.25 to 0.25
- docs: bfloat16 [512, 512], P('row'), may hold values from -0.059814453 to 0.099609375
- doc_labels: int32 [512, 8], replicated, may hold values from 0 to 524287
Outputs:
- hidden: bfloat16 [524288, 512], P(('row', 'col'))
- grad_docs: float32 [512, 512], P('row')
- grad_weight: float32 [512, 512], replicated
Inputs may be any that keep to these rules, and one draw needn't show every extreme that they name: For each sending device and each column of its row, the used slots (msg_dst below 16) come first and 16 marks an unused slot. In every row of devices some column receives all 4 slots used from every sender of that row.
All inputs are finite; a program needn't handle non-finite values.
Results may differ from a plain program's by a relative error of at most 0.0052.
Values may be sent and summed in bfloat16 or wider, within the bound.
No kernel may reach another device: no remote copies, remote signals or barrier semaphores. Data moves between devices by JAX's collectives and lax.ppermute only.
A program may use at most 192 MiB of HBM per device.

v0:
```python
import jax
import jax.numpy as jnp
from jax import lax
from jax.sharding import PartitionSpec as P


def per_device(emb, tiles, msg_src, msg_dst, msg_count, weight, docs, doc_labels):
    n_col = lax.axis_size("col")
    n_row = lax.axis_size("row")
    label_dev, width = emb.shape
    blk = tiles.shape[-1]
    cap = tiles.shape[1]
    blk_dev = label_dev // blk
    labels_total = float(label_dev * n_row * n_col)
    pos_count = doc_labels.shape[1]
    own_blocks = emb.reshape(blk_dev, blk, width)
    picked = own_blocks[msg_src]
    messages = jnp.einsum(
        "pqij,pqjd->pqid", tiles, picked, preferred_element_type=jnp.float32
    ).astype(jnp.bfloat16)
    received, dst_seen, cnt_seen = (
        lax.all_to_all(messages, "col", split_axis=0, concat_axis=0, tiled=True),
        lax.all_to_all(
            msg_dst.astype(jnp.bfloat16), "col", split_axis=0, concat_axis=0, tiled=True
        ),
        lax.all_to_all(
            msg_count.astype(jnp.bfloat16), "col", split_axis=0, concat_axis=0, tiled=True
        ),
    )
    slots_all = n_col * cap
    block_ids = jnp.arange(blk_dev, dtype=jnp.float32)
    hot = (dst_seen.astype(jnp.float32).reshape(1, slots_all) == block_ids[:, None]).astype(
        jnp.float32
    )
    weighted = hot * cnt_seen.astype(jnp.float32).reshape(1, slots_all)
    total = jnp.dot(
        weighted.astype(jnp.bfloat16),
        received.reshape(slots_all, blk * width),
        preferred_element_type=jnp.float32,
    ).reshape(blk_dev, blk, width)
    total = total + float(blk) * own_blocks.astype(jnp.float32)
    denom = float(blk) + jnp.sum(weighted, axis=1)
    agg = (total / denom[:, None, None]).astype(jnp.bfloat16).reshape(label_dev, width)
    pre = jnp.dot(agg, weight, preferred_element_type=jnp.float32)
    hidden = jax.nn.silu(pre).astype(jnp.bfloat16)
    device = lax.axis_index("row") * n_col + lax.axis_index("col")
    label_ids = device * label_dev + jnp.arange(label_dev, dtype=jnp.int32)
    piece = lax.all_gather(docs, "row", axis=0, tiled=True)
    scores = jnp.einsum("nd,ld->nl", piece, hidden, preferred_element_type=jnp.float32)
    positive = doc_labels[:, 0:1] == label_ids[None, :]
    for which in range(1, pos_count):
        positive = positive | (doc_labels[:, which : which + 1] == label_ids[None, :])
    prob = jax.nn.sigmoid(scores)
    dscore = jnp.where(positive, (prob - 1.0) / float(pos_count), prob / labels_total).astype(
        jnp.bfloat16
    )
    rows_grad = jnp.dot(dscore, hidden, preferred_element_type=jnp.float32)
    dhid = jnp.einsum("nl,nd->ld", dscore, piece, preferred_element_type=jnp.float32)
    doc_grad = rows_grad
    dhid, doc_grad = (dhid, doc_grad)
    sig = jax.nn.sigmoid(pre)
    dpre = (dhid * sig * (1.0 + pre * (1.0 - sig))).astype(jnp.bfloat16)
    weight_part = jnp.einsum("la,lb->ab", agg, dpre, preferred_element_type=jnp.float32)
    grad_weight = lax.psum(weight_part, ("row", "col"))
    row_share = lax.psum_scatter(doc_grad, "row", scatter_dimension=0, tiled=True)
    grad_docs = lax.psum(row_share, "col")
    return (hidden, grad_docs, grad_weight)


def solution(mesh):
    in_specs = (
        P(("row", "col"), None),
        P(("row", "col"), None, None, None),
        P(("row", "col"), None),
        P(("row", "col"), None),
        P(("row", "col"), None),
        P(),
        P("row", None),
        P(),
    )
    out_specs = (P(("row", "col"), None), P("row", None), P())
    return jax.shard_map(
        per_device, mesh=mesh, in_specs=in_specs, out_specs=out_specs, check_vma=False
    )
```

profile of v0, /device:TPU:0, one launch (start us, length us, event | category | flops | bytes accessed | tf_op | source)
XLA Modules:
  0.0 621.5 jit_solution(9641399624754386184)
XLA Ops:
  8.0 0.0 copy-start
  8.0 0.7 convert_bitcast_fusion.2
  8.8 0.7 copy.23
  9.5 7.1 %all-to-all-start = ((bf16[16,1,4]{2,1,0:T(2,128)(2,1)}), bf16[16,1,4]{2,1,0:T(2,128)(2,1)S(1)}, u32[]{:S(2)}, u32[]{:S(2)}) async-start(bf16[16,1,4]{2,1,0:T(2,128)(2,1)} %copy.23), calls=%async_computation | async-start | bytes 16384 | tf_op jit(solution)/shard_map/all_to_all | solution.py:23
  16.6 0.7 convert_bitcast_fusion.1
  17.3 0.7 copy.24
  18.0 0.7 compare_select_fusion
  18.7 0.1 copy.25
  18.8 0.1 reshape.51
  18.9 9.8 %gather_fusion = bf16[64,256,512]{2,1,0:T(8,128)(2,1)} fusion(bf16[16,256,512]{2,1,0:T(8,128)(2,1)} %bitcast.53, s32[1024]{0:T(1024)S(1)} %pad_clamp_fusion), kind=kCustom, calls=%fused_computation | custom fusion | bytes 33554688 | tf_op jit(solution)/shard_map/gather | solution.py:17
  28.6 0.0 all-to-all-done
  28.6 7.2 %all-to-all-start.1 = ((bf16[16,1,4]{2,1,0:T(2,128)(2,1)}), bf16[16,1,4]{2,1,0:T(2,128)(2,1)S(1)}, u32[]{:S(2)}, u32[]{:S(2)}) async-start(bf16[16,1,4]{2,1,0:T(2,128)(2,1)} %copy.24), calls=%async_computation.1 | async-start | bytes 16384 | tf_op jit(solution)/shard_map/all_to_all | solution.py:26
  35.9 19.3 %convert_bitcast_fusion = bf16[16,4,256,512]{2,3,1,0:T(8,128)(2,1)} fusion(bf16[16,4,256,512]{3,2,1,0:T(8,128)(2,1)} %bitcast.52, bf16[16,4,256,256]{3,2,1,0:T(8,128)(2,1)} %param.9), kind=kOutput, calls=%fused_computation.4 | convolution fusion | flops 4303355904 | bytes 41943040 | tf_op jit(solution)/shard_map/pqij,pqjd->pqid/dot_general | solution.py:18
  55.1 0.0 copy-start.6
  55.1 0.0 copy-start.5
  55.1 0.0 all-to-all-done.1
  55.1 7.4 %all-to-all-start.2 = ((bf16[16,4,256,512]{2,3,1,0:T(8,128)(2,1)}), bf16[16,4,256,512]{2,3,1,0:T(8,128)(2,1)}, u32[]{:S(2)}, u32[]{:S(2)}) async-start(bf16[16,4,256,512]{2,3,1,0:T(8,128)(2,1)} %convert_bitcast_fusion), calls=%async_computation.2 | async-start | bytes 33554432 | tf_op jit(solution)/shard_map/all_to_all | solution.py:22
  62.6 0.0 reduce-scatter.2.cloned.1.call-start
  62.6 0.0 copy-done.6
  62.7 0.0 copy-done.5
  62.7 14.5 %all_gather.3 = bf16[512,512]{1,0:T(8,128)(2,1)S(1)} all-gather(bf16[64,512]{1,0:T(8,128)(2,1)S(1)} %copy-done.5), channel_id=1, replica_groups=mesh['row'=8,'col'=16] {'row'}, dimensions={0}, use_global_device_ids=true | all-gather | bytes 589824 | tf_op jit(solution)/shard_map/all_gather | solution.py:48
  77.2 0.1 reshape.47
  77.3 0.1 reshape.48
  77.4 0.1 select_reduce_fusion
  77.5 229.1 %all-to-all-done.2 = bf16[16,4,256,512]{2,3,1,0:T(8,128)(2,1)} async-done(((bf16[16,4,256,512]{2,3,1,0:T(8,128)(2,1)}), bf16[16,4,256,512]{2,3,1,0:T(8,128)(2,1)}, u32[]{:S(2)}, u32[]{:S(2)}) %all-to-all-start.2) | async-done | bytes 16777248 | tf_op jit(solution)/shard_map/all_to_all | solution.py:22
  306.7 24.3 %copy.33 = bf16[8,8,256,512]{3,1,2,0:T(8,128)(2,1)} copy(bf16[8,8,256,512]{2,3,1,0:T(8,128)(2,1)} %bitcast.36) | data formatting | bytes 33554432
  331.0 9.2 %divide_convert_fusion = bf16[16,256,512]{2,0,1:T(8,128)(2,1)S(1)} fusion(bf16[16,256,512]{2,1,0:T(8,128)(2,1)} %bitcast.54, f32[16]{0:T(128)S(1)} %broadcast_add_fusion, f32[64]{0:T(128)S(1)} %reshape.48, f32[64]{0:T(128)S(1)} %reshape.47, bf16[8,8,256,512]{3,1,2,0:T(8,128)(2,1)} %copy.33), kind=kOutput, calls=%fused_computation.10 | convolution fusion | flops 278923264 | bytes 25166400 | tf_op jit(solution)/shard_map/dot_general | solution.py:36
  340.2 2.4 copy.30
  342.6 0.0 copy-start.4
  342.6 0.0 copy-done
  342.6 5.7 multiply_convert_fusion.1
  348.3 0.0 copy-done.4
  348.3 0.0 copy-start.2
  348.3 10.1 %fusion.3 = bf16[512,4096]{0,1:T(8,128)(2,1)S(1)} fusion(bf16[4096,512]{1,0:T(8,128)(2,1)S(1)} %get-tuple-element.13, bf16[512,512]{1,0:T(8,128)(2,1)S(1)} %all_gather.3, s32[512]{0:T(512)S(1)} %bitcast.63, s32[512]{0:T(512)S(1)} %bitcast.64, s32[512]{0:T(512)S(1)} %bitcast.58, s32[512]{0:T(512)S(1)} %bitcast.59, s32[512]{0:T(512)S(1)} %bitcast.60, ...), kind=kOutput, calls=%fused_computation.6 | convolution fusion | flops 2195718144 | bytes 8945664 | tf_op jit(solution)/shard_map/nd,ld->nl/dot_general | solution.py:49
  358.3 0.0 copy-done.2
  358.3 0.0 copy-start.3
  358.4 1.9 copy-done.3
  360.3 3.3 fusion.15
  363.6 0.0 reduce-scatter.2.cloned.1.call-update
  363.6 0.3 all-reduce.5.cloned.1.call-start
  363.9 0.0 copy-start.1
  363.9 12.6 %fusion.6 = f32[512,512]{1,0:T(8,128)} fusion(bf16[4096,512]{1,0:T(8,128)(2,1)} %bitcast.56, f32[4096,512]{1,0:T(8,128)} %get-tuple-element.12, bf16[512,4096]{0,1:T(8,128)(2,1)} %copy-done.3, bf16[512,512]{1,0:T(8,128)(2,1)S(1)} %all_gather.3), kind=kOutput, calls=%fused_computation.11 | convolution fusion | flops 4313841664 | bytes 18350080 | tf_op jit(solution)/shard_map/la,lb->ab/dot_general | solution.py:63
  376.5 0.0 all-reduce.5.cloned.1.call-update
  376.6 0.0 all-reduce.3.cloned.1.call-start
  376.6 21.8 %reduce-scatter.2.cloned.1.call-done = f32[64,512]{1,0:T(8,128)} async-done(((f32[512,512]{1,0:T(8,128)}), f32[64,512]{1,0:T(8,128)}) %reduce-scatter.2.cloned.1.call-update) | async-done | bytes 131088 | tf_op jit(solution)/shard_map/reduce_scatter | solution.py:65
  398.4 0.0 all-reduce.3.cloned.1.call-update
  398.5 127.3 %all-reduce.5.cloned.1.call-done = f32[512,512]{1,0:T(8,128)} async-done(((f32[512,512]{1,0:T(8,128)}), f32[512,512]{1,0:T(8,128)}) %all-reduce.5.cloned.1.call-update) | async-done | bytes 1048592 | tf_op jit(solution)/shard_map/psum | solution.py:64
  525.7 84.6 %all-reduce.3.cloned.1.call-done = f32[64,512]{1,0:T(8,128)} async-done(((f32[64,512]{1,0:T(8,128)}), f32[64,512]{1,0:T(8,128)}) %all-reduce.3.cloned.1.call-update) | async-done | bytes 131088 | tf_op jit(solution)/shard_map/psum | solution.py:66
  610.3 1.6 copy.44
  611.8 2.3 copy.45
  614.1 0.0 copy-done.1
  (6 shorter events, 0.1 us)
Async XLA Ops:
  8.0 334.6 %copy-start = (bf16[512,512]{1,0:T(8,128)(2,1)S(1)}, bf16[512,512]{1,0:T(8,128)(2,1)}, u32[]{:S(2)}) copy-start(bf16[512,512]{1,0:T(8,128)(2,1)} %param.13) | copy-start | bytes 1572868
  9.5 19.2 %all-to-all-start = ((bf16[16,1,4]{2,1,0:T(2,128)(2,1)}), bf16[16,1,4]{2,1,0:T(2,128)(2,1)S(1)}, u32[]{:S(2)}, u32[]{:S(2)}) async-start(bf16[16,1,4]{2,1,0:T(2,128)(2,1)} %copy.23), calls=%async_computation | async-start | bytes 16384 | tf_op jit(solution)/shard_map/all_to_all | solution.py:23
  28.6 26.5 %all-to-all-start.1 = ((bf16[16,1,4]{2,1,0:T(2,128)(2,1)}), bf16[16,1,4]{2,1,0:T(2,128)(2,1)S(1)}, u32[]{:S(2)}, u32[]{:S(2)}) async-start(bf16[16,1,4]{2,1,0:T(2,128)(2,1)} %copy.24), calls=%async_computation.1 | async-start | bytes 16384 | tf_op jit(solution)/shard_map/all_to_all | solution.py:26
  55.1 7.5 %copy-start.6 = (s32[512,8]{0,1:T(8,128)S(1)}, s32[512,8]{0,1:T(8,128)}, u32[]{:S(2)}) copy-start(s32[512,8]{0,1:T(8,128)} %param.15) | copy-start | bytes 49156
  55.1 7.5 %copy-start.5 = (bf16[64,512]{1,0:T(8,128)(2,1)S(1)}, bf16[64,512]{1,0:T(8,128)(2,1)}, u32[]{:S(2)}) copy-start(bf16[64,512]{1,0:T(8,128)(2,1)} %param.14) | copy-start | bytes 196612
  55.1 251.5 %all-to-all-start.2 = ((bf16[16,4,256,512]{2,3,1,0:T(8,128)(2,1)}), bf16[16,4,256,512]{2,3,1,0:T(8,128)(2,1)}, u32[]{:S(2)}, u32[]{:S(2)}) async-start(bf16[16,4,256,512]{2,3,1,0:T(8,128)(2,1)} %convert_bitcast_fusion), calls=%async_computation.2 | async-start | bytes 33554432 | tf_op jit(solution)/shard_map/all_to_all | solution.py:22
  62.6 335.9 %reduce-scatter.2.cloned.1.call-start = ((), (), s32[]{:S(2)}) async-start(), calls=%async_computation.4 | async-start | bytes 1179648 | tf_op jit(solution)/shard_map/reduce_scatter | solution.py:65
  342.6 5.7 copy-start.4
  348.3 10.1 %copy-start.2 = (bf16[4096,512]{1,0:T(8,128)(2,1)}, bf16[4096,512]{1,0:T(8,128)(2,1)S(1)}, u32[]{:S(2)}) copy-start(bf16[4096,512]{1,0:T(8,128)(2,1)S(1)} %get-tuple-element.13) | copy-start | bytes 12582916
  358.3 1.9 copy-start.3
  363.6 162.1 %all-reduce.5.cloned.1.call-start = ((), (), s32[]{:S(2)}) async-start(), calls=%async_computation.6 | async-start | bytes 2097152 | tf_op jit(solution)/shard_map/psum | solution.py:64
  363.9 250.2 %copy-start.1 = (bf16[512,512]{1,0:T(8,128)(2,1)S(1)}, bf16[512,512]{1,0:T(8,128)(2,1)}, u32[]{:S(2)}) copy-start(bf16[512,512]{1,0:T(8,128)(2,1)} %param.13) | copy-start | bytes 1572868
  376.6 233.7 %all-reduce.3.cloned.1.call-start = ((), (), s32[]{:S(2)}) async-start(), calls=%async_computation.5 | async-start | bytes 262144 | tf_op jit(solution)/shard_map/psum | solution.py:66
Sparse Core Ops, SparseCore 0:
  363.8 34.6 reduce-scatter.1
Sparse Core Ops, SparseCore 1:
  376.6 149.0 all-reduce.4
  528.8 81.4 all-reduce.2
where the time goes:
time: 623 us; the launch traced here: 622 us
  waiting for transfers between devices  463 us (74%)
  matrix products  60.1 us (10%)
  local copies, waits for them, and re-layouts  44 us (7%)
  starting transfers between devices  22.1 us (4%)
  between operations  15.7 us (3%)
  blocking collectives  14.5 us (2%)
    all_to_all x1, waiting for transfers between devices, per_device(): lax.all_to_all(messages, 'col', split_axis=0, concat_axis=0, tiled=True)  229 us
    psum x1, waiting for transfers between devices, per_device(): grad_weight = lax.psum(weight_part, ('row', 'col'))  127 us
    psum x1, waiting for transfers between devices, per_device(): grad_docs = lax.psum(row_share, 'col')  84.6 us
    unnamed x17, local copies, waits for them, and re-layouts  30.1 us
    reduce_scatter x1, waiting for transfers between devices, per_device(): lax.psum_scatter(doc_grad, 'row', scatter_dimension=0, tiled=True)  21.8 us
    dot_general x1, matrix products, per_device(): jnp.einsum('pqij,pqjd->pqid', tiles, picked, preferred_element_type=jnp.f...  19.3 us
    all_gather x1, blocking collectives, per_device(): piece = lax.all_gather(docs, 'row', axis=0, tiled=True)  14.5 us
    dot_general x1, matrix products, per_device(): jnp.einsum('la,lb->ab', agg, dpre, preferred_element_type=jnp.float32)  12.6 us
  transfers between devices with their start and end apart: 6, of which 4 were waited for; matrix products, arithmetic and copies ran while one was open for 7% of the time, Pallas kernels for 0%

commit v1 on v0

--- a/solution.py
+++ b/solution.py
@@ -61,7 +61,7 @@
     sig = jax.nn.sigmoid(pre)
     dpre = (dhid * sig * (1.0 + pre * (1.0 - sig))).astype(jnp.bfloat16)
     weight_part = jnp.einsum("la,lb->ab", agg, dpre, preferred_element_type=jnp.float32)
-    grad_weight = lax.psum(weight_part, ("row", "col"))
+    grad_weight = lax.psum(lax.psum(weight_part, "col"), "row")
     row_share = lax.psum_scatter(doc_grad, "row", scatter_dimension=0, tiled=True)
     grad_docs = lax.psum(row_share, "col")
     return (hidden, grad_docs, grad_weight)

time: 623 us -> 562 us (0.902)
  waiting for transfers between devices: 463 us -> 404 us
    psum x1, waiting for transfers between devices: 127 us -> 64.4 us  [per_device(): grad_weight = lax.psum(lax.psum(weight_part, 'col'), 'row')]
  transfers between devices with their start and end apart: 6 -> 6, of which waited for: 4 -> 4; matrix products, arithmetic and copies ran while one was open for 7% -> 8% of each run, Pallas kernels for 0% -> 0%
where the time goes in v1:
time: 562 us; the launch traced here: 561 us
  waiting for transfers between devices  404 us (72%)
  matrix products  60.1 us (11%)
  local copies, waits for them, and re-layouts  44 us (8%)
  starting transfers between devices  22.1 us (4%)
  blocking collectives  14.5 us (3%)
  between operations  13.9 us (2%)
    all_to_all x1, waiting for transfers between devices, per_device(): lax.all_to_all(messages, 'col', split_axis=0, concat_axis=0, tiled=True)  229 us
    psum x1, waiting for transfers between devices, per_device(): grad_docs = lax.psum(row_share, 'col')  89 us
    psum x1, waiting for transfers between devices, per_device(): grad_weight = lax.psum(lax.psum(weight_part, 'col'), 'row')  64.4 us
    unnamed x17, local copies, waits for them, and re-layouts  30.1 us
    reduce_scatter x1, waiting for transfers between devices, per_device(): lax.psum_scatter(doc_grad, 'row', scatter_dimension=0, tiled=True)  21.5 us
    dot_general x1, matrix products, per_device(): jnp.einsum('pqij,pqjd->pqid', tiles, picked, preferred_element_type=jnp.f...  19.3 us
    all_gather x1, blocking collectives, per_device(): piece = lax.all_gather(docs, 'row', axis=0, tiled=True)  14.5 us
    dot_general x1, matrix products, per_device(): jnp.einsum('la,lb->ab', agg, dpre, preferred_element_type=jnp.float32)  12.6 us
  transfers between devices with their start and end apart: 6, of which 4 were waited for; matrix products, arithmetic and copies ran while one was open for 8% of the time, Pallas kernels for 0%

profile of v1, /device:TPU:0, one launch (start us, length us, event | category | flops | bytes accessed | tf_op | source)
XLA Modules:
  0.0 561.1 jit_solution(8395262945396128657)
XLA Ops:
  7.2 0.0 copy-start
  7.2 0.7 convert_bitcast_fusion.2
  7.9 0.7 copy.23
  8.6 7.1 %all-to-all-start = ((bf16[16,1,4]{2,1,0:T(2,128)(2,1)}), bf16[16,1,4]{2,1,0:T(2,128)(2,1)S(1)}, u32[]{:S(2)}, u32[]{:S(2)}) async-start(bf16[16,1,4]{2,1,0:T(2,128)(2,1)} %copy.23), calls=%async_computation | async-start | bytes 16384 | tf_op jit(solution)/shard_map/all_to_all | solution.py:23
  15.8 0.7 convert_bitcast_fusion.1
  16.5 0.7 copy.24
  17.2 0.7 compare_select_fusion
  17.8 0.1 copy.25
  17.9 0.1 reshape.51
  18.0 9.8 %gather_fusion = bf16[64,256,512]{2,1,0:T(8,128)(2,1)} fusion(bf16[16,256,512]{2,1,0:T(8,128)(2,1)} %bitcast.53, s32[1024]{0:T(1024)S(1)} %pad_clamp_fusion), kind=kCustom, calls=%fused_computation | custom fusion | bytes 33554688 | tf_op jit(solution)/shard_map/gather | solution.py:17
  27.8 0.0 all-to-all-done
  27.8 7.2 %all-to-all-start.1 = ((bf16[16,1,4]{2,1,0:T(2,128)(2,1)}), bf16[16,1,4]{2,1,0:T(2,128)(2,1)S(1)}, u32[]{:S(2)}, u32[]{:S(2)}) async-start(bf16[16,1,4]{2,1,0:T(2,128)(2,1)} %copy.24), calls=%async_computation.1 | async-start | bytes 16384 | tf_op jit(solution)/shard_map/all_to_all | solution.py:26
  35.0 19.3 %convert_bitcast_fusion = bf16[16,4,256,512]{2,3,1,0:T(8,128)(2,1)} fusion(bf16[16,4,256,512]{3,2,1,0:T(8,128)(2,1)} %bitcast.52, bf16[16,4,256,256]{3,2,1,0:T(8,128)(2,1)} %param.9), kind=kOutput, calls=%fused_computation.4 | convolution fusion | flops 4303355904 | bytes 41943040 | tf_op jit(solution)/shard_map/pqij,pqjd->pqid/dot_general | solution.py:18
  54.3 0.0 copy-start.6
  54.3 0.0 copy-start.5
  54.3 0.0 all-to-all-done.1
  54.3 7.4 %all-to-all-start.2 = ((bf16[16,4,256,512]{2,3,1,0:T(8,128)(2,1)}), bf16[16,4,256,512]{2,3,1,0:T(8,128)(2,1)}, u32[]{:S(2)}, u32[]{:S(2)}) async-start(bf16[16,4,256,512]{2,3,1,0:T(8,128)(2,1)} %convert_bitcast_fusion), calls=%async_computation.2 | async-start | bytes 33554432 | tf_op jit(solution)/shard_map/all_to_all | solution.py:22
  61.7 0.0 reduce-scatter.2.cloned.1.call-start
  61.8 0.0 copy-done.6
  61.8 0.0 copy-done.5
  61.8 14.5 %all_gather.3 = bf16[512,512]{1,0:T(8,128)(2,1)S(1)} all-gather(bf16[64,512]{1,0:T(8,128)(2,1)S(1)} %copy-done.5), channel_id=1, replica_groups=mesh['row'=8,'col'=16] {'row'}, dimensions={0}, use_global_device_ids=true | all-gather | bytes 589824 | tf_op jit(solution)/shard_map/all_gather | solution.py:48
  76.3 0.1 reshape.47
  76.5 0.1 reshape.48
  76.5 0.1 select_reduce_fusion
  76.7 229.1 %all-to-all-done.2 = bf16[16,4,256,512]{2,3,1,0:T(8,128)(2,1)} async-done(((bf16[16,4,256,512]{2,3,1,0:T(8,128)(2,1)}), bf16[16,4,256,512]{2,3,1,0:T(8,128)(2,1)}, u32[]{:S(2)}, u32[]{:S(2)}) %all-to-all-start.2) | async-done | bytes 16777248 | tf_op jit(solution)/shard_map/all_to_all | solution.py:22
  305.8 24.3 %copy.33 = bf16[8,8,256,512]{3,1,2,0:T(8,128)(2,1)} copy(bf16[8,8,256,512]{2,3,1,0:T(8,128)(2,1)} %bitcast.36) | data formatting | bytes 33554432
  330.1 9.2 %divide_convert_fusion = bf16[16,256,512]{2,0,1:T(8,128)(2,1)S(1)} fusion(bf16[16,256,512]{2,1,0:T(8,128)(2,1)} %bitcast.54, f32[16]{0:T(128)S(1)} %broadcast_add_fusion, f32[64]{0:T(128)S(1)} %reshape.48, f32[64]{0:T(128)S(1)} %reshape.47, bf16[8,8,256,512]{3,1,2,0:T(8,128)(2,1)} %copy.33), kind=kOutput, calls=%fused_computation.10 | convolution fusion | flops 278923264 | bytes 25166400 | tf_op jit(solution)/shard_map/dot_general | solution.py:36
  339.3 2.4 copy.30
  341.7 0.0 copy-start.4
  341.7 0.0 copy-done
  341.7 5.7 %multiply_convert_fusion.1 = (bf16[4096,512]{1,0:T(8,128)(2,1)S(1)}, f32[4096,512]{1,0:T(8,128)}) fusion(bf16[4096,512]{1,0:T(8,128)(2,1)S(1)} %bitcast.55, bf16[512,512]{1,0:T(8,128)(2,1)S(1)} %copy-done), kind=kOutput, calls=%fused_computation.8 | convolution fusion | flops 2157969408 | bytes 17301504 | tf_op jit(solution)/shard_map/dot_general | solution.py:44
  347.4 0.0 copy-done.4
  347.4 0.0 copy-start.2
  347.4 10.1 %fusion.3 = bf16[512,4096]{0,1:T(8,128)(2,1)S(1)} fusion(bf16[4096,512]{1,0:T(8,128)(2,1)S(1)} %get-tuple-element.15, bf16[512,512]{1,0:T(8,128)(2,1)S(1)} %all_gather.3, s32[512]{0:T(512)S(1)} %bitcast.63, s32[512]{0:T(512)S(1)} %bitcast.64, s32[512]{0:T(512)S(1)} %bitcast.58, s32[512]{0:T(512)S(1)} %bitcast.59, s32[512]{0:T(512)S(1)} %bitcast.60, ...), kind=kOutput, calls=%fused_computation.6 | convolution fusion | flops 2195718144 | bytes 8945664 | tf_op jit(solution)/shard_map/nd,ld->nl/dot_general | solution.py:49
  357.5 0.0 copy-done.2
  357.5 0.0 copy-start.3
  357.5 1.9 copy-done.3
  359.4 3.3 fusion.15
  362.7 0.0 reduce-scatter.2.cloned.1.call-update
  362.7 0.3 all-reduce.6.cloned.1.call-start
  363.0 0.0 copy-start.1
  363.0 12.6 %fusion.6 = f32[512,512]{1,0:T(8,128)} fusion(bf16[4096,512]{1,0:T(8,128)(2,1)} %bitcast.56, f32[4096,512]{1,0:T(8,128)} %get-tuple-element.14, bf16[512,4096]{0,1:T(8,128)(2,1)} %copy-done.3, bf16[512,512]{1,0:T(8,128)(2,1)S(1)} %all_gather.3), kind=kOutput, calls=%fused_computation.11 | convolution fusion | flops 4313841664 | bytes 18350080 | tf_op jit(solution)/shard_map/la,lb->ab/dot_general | solution.py:63
  375.7 21.5 %reduce-scatter.2.cloned.1.call-done = f32[64,512]{1,0:T(8,128)} async-done(((f32[512,512]{1,0:T(8,128)}), f32[64,512]{1,0:T(8,128)}) %reduce-scatter.2.cloned.1.call-update) | async-done | bytes 131088 | tf_op jit(solution)/shard_map/reduce_scatter | solution.py:65
  397.1 0.0 all-reduce.6.cloned.1.call-update
  397.2 0.0 all-reduce.4.cloned.1.call-start
  397.2 89.0 %all-reduce.6.cloned.1.call-done = (f32[64,512]{1,0:T(8,128)}, f32[512,512]{1,0:T(8,128)}) async-done(((f32[64,512]{1,0:T(8,128)}, f32[512,512]{1,0:T(8,128)}), (f32[64,512]{1,0:T(8,128)}, f32[512,512]{1,0:T(8,128)})) %all-reduce.6.cloned.1.call-update) | async-done | bytes 1179664 | tf_op jit(solution)/shard_map/psum | solution.py:66
  486.2 0.0 all-reduce.4.cloned.1.call-update
  486.3 64.4 %all-reduce.4.cloned.1.call-done = f32[512,512]{1,0:T(8,128)} async-done(((f32[512,512]{1,0:T(8,128)}), f32[512,512]{1,0:T(8,128)}) %all-reduce.4.cloned.1.call-update) | async-done | bytes 1048592 | tf_op jit(solution)/shard_map/psum | solution.py:64
  550.7 1.6 copy.45
  552.3 2.3 copy.46
  554.5 0.0 copy-done.1
  (6 shorter events, 0.1 us)
Async XLA Ops:
  7.2 334.5 %copy-start = (bf16[512,512]{1,0:T(8,128)(2,1)S(1)}, bf16[512,512]{1,0:T(8,128)(2,1)}, u32[]{:S(2)}) copy-start(bf16[512,512]{1,0:T(8,128)(2,1)} %param.13) | copy-start | bytes 1572868
  8.6 19.2 %all-to-all-start = ((bf16[16,1,4]{2,1,0:T(2,128)(2,1)}), bf16[16,1,4]{2,1,0:T(2,128)(2,1)S(1)}, u32[]{:S(2)}, u32[]{:S(2)}) async-start(bf16[16,1,4]{2,1,0:T(2,128)(2,1)} %copy.23), calls=%async_computation | async-start | bytes 16384 | tf_op jit(solution)/shard_map/all_to_all | solution.py:23
  27.8 26.5 %all-to-all-start.1 = ((bf16[16,1,4]{2,1,0:T(2,128)(2,1)}), bf16[16,1,4]{2,1,0:T(2,128)(2,1)S(1)}, u32[]{:S(2)}, u32[]{:S(2)}) async-start(bf16[16,1,4]{2,1,0:T(2,128)(2,1)} %copy.24), calls=%async_computation.1 | async-start | bytes 16384 | tf_op jit(solution)/shard_map/all_to_all | solution.py:26
  54.3 7.5 %copy-start.6 = (s32[512,8]{0,1:T(8,128)S(1)}, s32[512,8]{0,1:T(8,128)}, u32[]{:S(2)}) copy-start(s32[512,8]{0,1:T(8,128)} %param.15) | copy-start | bytes 49156
  54.3 7.5 %copy-start.5 = (bf16[64,512]{1,0:T(8,128)(2,1)S(1)}, bf16[64,512]{1,0:T(8,128)(2,1)}, u32[]{:S(2)}) copy-start(bf16[64,512]{1,0:T(8,128)(2,1)} %param.14) | copy-start | bytes 196612
  54.3 251.5 %all-to-all-start.2 = ((bf16[16,4,256,512]{2,3,1,0:T(8,128)(2,1)}), bf16[16,4,256,512]{2,3,1,0:T(8,128)(2,1)}, u32[]{:S(2)}, u32[]{:S(2)}) async-start(bf16[16,4,256,512]{2,3,1,0:T(8,128)(2,1)} %convert_bitcast_fusion), calls=%async_computation.2 | async-start | bytes 33554432 | tf_op jit(solution)/shard_map/all_to_all | solution.py:22
  61.7 335.4 %reduce-scatter.2.cloned.1.call-start = ((), (), s32[]{:S(2)}) async-start(), calls=%async_computation.4 | async-start | bytes 1179648 | tf_op jit(solution)/shard_map/reduce_scatter | solution.py:65
  341.7 5.7 %copy-start.4 = (bf16[16,256,512]{2,1,0:T(8,128)(2,1)}, bf16[16,256,512]{2,1,0:T(8,128)(2,1)S(1)}, u32[]{:S(2)}) copy-start(bf16[16,256,512]{2,1,0:T(8,128)(2,1)S(1)} %copy.30) | copy-start | bytes 12582916
  347.4 10.1 %copy-start.2 = (bf16[4096,512]{1,0:T(8,128)(2,1)}, bf16[4096,512]{1,0:T(8,128)(2,1)S(1)}, u32[]{:S(2)}) copy-start(bf16[4096,512]{1,0:T(8,128)(2,1)S(1)} %get-tuple-element.15) | copy-start | bytes 12582916
  357.5 1.9 copy-start.3
  362.7 123.5 %all-reduce.6.cloned.1.call-start = ((), (), s32[]{:S(2)}) async-start(), calls=%async_computation.6 | async-start | bytes 2359296 | tf_op jit(solution)/shard_map/psum | solution.py:66
  363.0 191.5 %copy-start.1 = (bf16[512,512]{1,0:T(8,128)(2,1)S(1)}, bf16[512,512]{1,0:T(8,128)(2,1)}, u32[]{:S(2)}) copy-start(bf16[512,512]{1,0:T(8,128)(2,1)} %param.13) | copy-start | bytes 1572868
  397.2 153.5 %all-reduce.4.cloned.1.call-start = ((), (), s32[]{:S(2)}) async-start(), calls=%async_computation.5 | async-start | bytes 2097152 | tf_op jit(solution)/shard_map/psum | solution.py:64
Sparse Core Ops, SparseCore 0:
  362.9 34.2 reduce-scatter.1
  400.5 85.6 all-reduce.5
  488.6 62.0 all-reduce.3
